TPU v7x, 256 devices: a whole 4x4x8 slice. The times are simulated.
256 devices in a mesh: row: 16 (over y, x), col: 16 (over z, core).
Axes of the slice: x: 4, y: 4, z: 8, core: 2. Of those that a mesh axis runs over, the one named last changes fastest.
Arguments:
- hidden_in: bfloat16 [1024, 4096], P('col', 'row'), may hold values from -250 to 250
- norm_gain: bfloat16 [4096], P('row'), may hold values from 0.099609375 to 1.8984375
- w_qkv: bfloat16 [4096, 6144], P('row', 'col'), may hold values from -0.125 to 0.125
- w_out: bfloat16 [4096, 4096], P('row', 'col'), may hold values from -0.125 to 0.125
- cache_k: bfloat16 [16, 4096, 1024], P('col', 'row'), may hold values from -1300 to 1300
- value_cache: bfloat16 [16, 4096, 1024], P('col', 'row'), may hold values from -6 to 6
- cache_len: int32 [16], P('col'), may hold values from 1 to 4096, as said below
- parents: int32 [16, 64], P('col'), may hold values from -1 to 62, as said below
Outputs:
- update: bfloat16 [1024, 4096], P('col', 'row')
Inputs may be any that keep to these rules, and one draw needn't show every extreme that they name: Slots 0 to cache_len - 1 of a request's window are filled; some request fills all 4096 slots. `parents`: slot 0 of every request is the root with parent -1; every other slot's parent is an earlier slot of the same request; slot 63 has parent 64 - 2.
All inputs are finite; a program needn't handle non-finite values.
Results may differ from a plain program's by a relative error of at most 0.011.
The roundings to bfloat16 on the way count: a program that leaves them out, or rounds other values in their place, can miss the bound.
Values may be sent and summed in bfloat16 or wider, within the bound.
A program may use at most 128 MiB of HBM per device.

v0:
```python
import jax
import jax.numpy as jnp
from jax import lax
from jax.sharding import PartitionSpec as P

D = 4096
QUERY_HEADS = 32
KEY_VALUE_HEADS = 8
HEAD_SIZE = 128
masked_score = -1e30


def merged(value, axis, join):
    pieces = jax.tree.map(lambda part: lax.all_gather(part, axis), value)
    head = jax.tree.map(lambda part: part[0], pieces)
    tail = jax.tree.map(lambda part: part[1:], pieces)
    so_far, _ = lax.scan(lambda so_far, piece: (join(so_far, piece), None), head, tail)
    return so_far


def ancestors(parents):
    draft_tree = parents.shape[1]
    slot_ids = jnp.arange(draft_tree, dtype=jnp.int32)
    parent_links = (parents[:, :, None] == slot_ids[None, None, :]).astype(jnp.float32)
    reachable = parent_links + jnp.eye(draft_tree, dtype=jnp.float32)[None]
    for squaring in range(max(1, (draft_tree - 1).bit_length())):
        product = jnp.einsum("rij,rjk->rik", reachable, reachable, precision=lax.Precision.HIGHEST)
        reachable = (product > 0.5).astype(jnp.float32)
    return reachable > 0.5


def pair_merge(first, second):
    peak = jnp.maximum(first[0], second[0])
    first_scale = jnp.exp(first[0] - peak)
    second_scale = jnp.exp(second[0] - peak)
    totals = first[1] * first_scale + second[1] * second_scale
    blended = first[2] * first_scale[..., None] + second[2] * second_scale[..., None]
    return (peak, totals, blended)


def shards(hidden_in, norm_gain, w_qkv, w_out, cache_k, value_cache, cache_len, parents):
    rows_here = hidden_in.shape[0]
    request_list = cache_k.shape[0]
    token_positions = cache_k.shape[1]
    draft_tree = parents.shape[1]
    head_groups = QUERY_HEADS // KEY_VALUE_HEADS
    heads_dev = QUERY_HEADS // lax.axis_size("row")
    row_index = lax.axis_index("row")
    score_scale = HEAD_SIZE ** (-0.5)
    features = hidden_in.astype(jnp.float32)
    squares = lax.psum(jnp.sum(features * features, axis=1), "row")
    row_scale = lax.rsqrt(squares / D + 1e-05)
    normed = (features * row_scale[:, None] * norm_gain.astype(jnp.float32)[None, :]).astype(
        jnp.bfloat16
    )
    partial_value = jnp.dot(
        normed, lax.all_gather(w_qkv, "col", axis=1, tiled=True), preferred_element_type=jnp.float32
    )
    summed = lax.psum_scatter(partial_value, "row", scatter_dimension=1, tiled=True).astype(
        jnp.bfloat16
    )
    projected_output = lax.all_gather(summed, "row", axis=1, tiled=True)
    query_block = projected_output[:, : QUERY_HEADS * HEAD_SIZE].reshape(
        request_list, draft_tree, KEY_VALUE_HEADS, head_groups, HEAD_SIZE
    )
    new_key_block = projected_output[
        :, QUERY_HEADS * HEAD_SIZE : (QUERY_HEADS + KEY_VALUE_HEADS) * HEAD_SIZE
    ].reshape(request_list, draft_tree, KEY_VALUE_HEADS, HEAD_SIZE)
    new_value_block = projected_output[:, (QUERY_HEADS + KEY_VALUE_HEADS) * HEAD_SIZE :].reshape(
        request_list, draft_tree, KEY_VALUE_HEADS, HEAD_SIZE
    )
    first_slot = row_index * token_positions
    slot_ids = first_slot + jnp.arange(token_positions, dtype=jnp.int32)

    def cache_part(request_item):
        query_rows, cached_key_rows, cached_value_rows, length = request_item
        key_row_block = cached_key_rows.reshape(token_positions, KEY_VALUE_HEADS, HEAD_SIZE)
        value_row_block = cached_value_rows.reshape(token_positions, KEY_VALUE_HEADS, HEAD_SIZE)
        scores = (
            jnp.einsum(
                "tkgd,pkd->kgtp", query_rows, key_row_block, preferred_element_type=jnp.float32
            )
            * score_scale
        )
        visible = (slot_ids < length)[None, None, None, :]
        scores = jnp.where(visible, scores, masked_score)
        highest = jnp.max(scores, axis=-1)
        weights = jnp.where(visible, jnp.exp(scores - highest[..., None]), 0.0)
        totals = jnp.sum(weights, axis=-1)
        blended = jnp.einsum(
            "kgtp,pkd->kgtd",
            weights.astype(jnp.bfloat16),
            value_row_block,
            preferred_element_type=jnp.float32,
        )
        return (
            highest.reshape(QUERY_HEADS, draft_tree),
            totals.reshape(QUERY_HEADS, draft_tree),
            blended.reshape(QUERY_HEADS, draft_tree, HEAD_SIZE),
        )

    maxima, totals, blended = lax.map(cache_part, (query_block, cache_k, value_cache, cache_len))
    maxima, totals, blended = merged((maxima, totals, blended), "row", pair_merge)
    max_own = lax.dynamic_slice_in_dim(maxima, row_index * heads_dev, heads_dev, 1)
    total_own = lax.dynamic_slice_in_dim(totals, row_index * heads_dev, heads_dev, 1)
    blend_own = lax.dynamic_slice_in_dim(blended, row_index * heads_dev, heads_dev, 1)
    allowed = ancestors(parents)[:, None, :, :]
    query_heads = projected_output[:, : QUERY_HEADS * HEAD_SIZE].reshape(
        request_list, draft_tree, QUERY_HEADS, HEAD_SIZE
    )
    query_own = lax.dynamic_slice_in_dim(query_heads, row_index * heads_dev, heads_dev, 2)
    key_own = lax.dynamic_slice_in_dim(
        jnp.repeat(new_key_block, head_groups, axis=2), row_index * heads_dev, heads_dev, 2
    )
    value_own = lax.dynamic_slice_in_dim(
        jnp.repeat(new_value_block, head_groups, axis=2), row_index * heads_dev, heads_dev, 2
    )
    tree_scores = (
        jnp.einsum("rthd,rshd->rhts", query_own, key_own, preferred_element_type=jnp.float32)
        * score_scale
    )
    tree_scores = jnp.where(allowed, tree_scores, masked_score)
    tree_max = jnp.max(tree_scores, axis=-1)
    tree_weights = jnp.where(allowed, jnp.exp(tree_scores - tree_max[..., None]), 0.0)
    tree_total = jnp.sum(tree_weights, axis=-1)
    tree_blend = jnp.einsum(
        "rhts,rshd->rhtd",
        tree_weights.astype(jnp.bfloat16),
        value_own,
        preferred_element_type=jnp.float32,
    )
    joint_max = jnp.maximum(max_own, tree_max)
    cache_scale = jnp.exp(max_own - joint_max)
    tree_scale = jnp.exp(tree_max - joint_max)
    numerator = blend_own * cache_scale[..., None] + tree_blend * tree_scale[..., None]
    denominator = total_own * cache_scale + tree_total * tree_scale
    attended = (numerator / denominator[..., None]).astype(jnp.bfloat16)
    attended = attended.transpose(0, 2, 1, 3).reshape(rows_here, heads_dev * HEAD_SIZE)
    partial_out = jnp.dot(
        attended,
        lax.all_gather(w_out, "col", axis=1, tiled=True),
        preferred_element_type=jnp.float32,
    )
    return lax.psum_scatter(partial_out, "row", scatter_dimension=1, tiled=True).astype(
        jnp.bfloat16
    )


def solution(mesh):
    placed = (
        P("col", "row"),
        P("row"),
        P("row", "col"),
        P("row", "col"),
        P("col", "row", None),
        P("col", "row", None),
        P("col"),
        P("col", None),
    )
    return jax.shard_map(
        shards, mesh=mesh, in_specs=placed, out_specs=P("col", "row"), check_vma=False
    )
```

profile of v0, /device:TPU:2, one launch (start us, length us, event | category | flops | bytes accessed | tf_op | source)
XLA Modules:
  0.0 420.8 jit_solution(8517399735573453257)
XLA Ops:
  8.8 37.7 %psum.7 = f32[64]{0:T(128)S(1)} all-reduce(f32[64]{0:T(128)S(1)} %fusion.29), channel_id=1, replica_groups=mesh['row'=16,'col'=16] {'row'}, use_global_device_ids=true, to_apply=%region_1.0 | all-reduce | flops 64 | bytes 512 | tf_op jit(solution)/shard_map/psum | solution.py:51
  46.5 6.5 %all-gather.4.cloned.1.call-done = bf16[256,6144]{1,0:T(8,128)(2,1)} async-done(((bf16[256,384]{1,0:T(8,128)(2,1)}), bf16[256,6144]{1,0:T(8,128)(2,1)}) %all-gather.4.cloned.1.call-update) | async-done | bytes 3145744 | tf_op jit(solution)/shard_map/all_gather | solution.py:57
  53.0 3.8 fusion.35
  59.3 75.1 %reduce-scatter.3.cloned.1.call-done = f32[64,384]{1,0:T(8,128)} async-done(((f32[64,6144]{1,0:T(8,128)}), f32[64,384]{1,0:T(8,128)}) %reduce-scatter.3.cloned.1.call-update) | async-done | bytes 98320 | tf_op jit(solution)/shard_map/reduce_scatter | solution.py:59
  135.3 22.6 %all_gather.28 = bf16[64,6144]{1,0:T(8,128)(2,1)S(1)} all-gather(bf16[64,384]{1,0:T(8,128)(2,1)S(1)} %convert_element_type.85), channel_id=1, replica_groups=mesh['row'=16,'col'=16] {'row'}, dimensions={1}, use_global_device_ids=true | all-gather | bytes 835584 | tf_op jit(solution)/shard_map/all_gather | solution.py:62
  165.5 24.1 %all_gather.32 = f32[16,1,32,64]{3,2,1,0:T(8,128)S(1)} all-gather(f32[1,1,32,64]{3,2,1,0:T(8,128)S(1)} %bitcast.147), channel_id=1, replica_groups=mesh['row'=16,'col'=16] {'row'}, dimensions={0}, use_global_device_ids=true | all-gather | bytes 139264 | tf_op jit(solution)/shard_map/all_gather | solution.py:14
  189.6 22.0 %all_gather.30 = f32[16,1,32,64]{3,2,1,0:T(8,128)S(1)} all-gather(f32[1,1,32,64]{3,2,1,0:T(8,128)S(1)} %bitcast.146), channel_id=1, replica_groups=mesh['row'=16,'col'=16] {'row'}, dimensions={0}, use_global_device_ids=true | all-gather | bytes 139264 | tf_op jit(solution)/shard_map/all_gather | solution.py:14
  212.2 68.4 %all-gather.6.cloned.1.call-done = f32[16,1,32,64,128]{4,3,2,1,0:T(8,128)} async-done(((f32[1,1,32,64,128]{4,3,2,1,0:T(8,128)}), f32[16,1,32,64,128]{4,3,2,1,0:T(8,128)}) %all-gather.6.cloned.1.call-update) | async-done | bytes 16777232 | tf_op jit(solution)/shard_map/all_gather | solution.py:14
  281.9 14.5 %slice.43 = f32[15,1,32,64,128]{4,3,2,1,0:T(8,128)} slice(f32[16,1,32,64,128]{4,3,2,1,0:T(8,128)} %all-gather.6.cloned.1.call-done), slice={[1:16], [0:1], [0:32], [0:64], [0:128]} | slice | bytes 31457280 | tf_op jit(solution)/shard_map/slice | solution.py:16
  296.5 34.1 %while.2 = (s32[]{:T(128)}, f32[1,32,64]{2,1,0:T(8,128)S(1)}, f32[1,32,64]{2,1,0:T(8,128)S(1)}, f32[1,32,64,128]{3,2,1,0:T(8,128)S(1)}, f32[15,1,32,64]{3,2,1,0:...) while((s32[]{:T(128)}, f32[1,32,64]{2,1,0:T(8,128)S(1)}, ...), condition=%wide.region_6.7_spmd, body=%wide.region_5.6_spmd.sunk | while | flops 800770 | bytes 3268713 | solution.py:17
  296.5 2.2 fusion.83
  298.8 2.2 fusion.83
  301.1 2.2 fusion.83
  303.4 2.2 fusion.83
  305.6 2.2 fusion.83
  307.9 2.2 fusion.83
  310.2 2.2 fusion.83
  312.5 2.2 fusion.83
  314.7 2.2 fusion.83
  317.0 2.2 fusion.83
  319.3 2.2 fusion.83
  321.6 2.2 fusion.83
  331.0 3.0 fusion.38
  334.1 78.7 %reduce-scatter.5.cloned.1.call-done = f32[64,256]{1,0:T(8,128)} async-done(((f32[64,4096]{1,0:T(8,128)}), f32[64,256]{1,0:T(8,128)}) %reduce-scatter.5.cloned.1.call-update) | async-done | bytes 65552 | tf_op jit(solution)/shard_map/reduce_scatter | solution.py:144
  (104 shorter events, 23.4 us)
Async XLA Ops:
  6.5 46.5 %all-gather.4.cloned.1.call-start = ((), (), s32[]{:S(2)}) async-start(), calls=%async_computation.2 | async-start | bytes 3342336 | tf_op jit(solution)/shard_map/all_gather | solution.py:57
  7.3 127.2 %reduce-scatter.3.cloned.1.call-start = ((), (), s32[]{:S(2)}) async-start(), calls=%async_computation.3 | async-start | bytes 1671168 | tf_op jit(solution)/shard_map/reduce_scatter | solution.py:59
  46.5 11.0 %copy-start = (bf16[1,256,1024]{2,1,0:T(8,128)(2,1)S(1)}, bf16[1,256,1024]{2,1,0:T(8,128)(2,1)}, u32[]{:S(2)}) copy-start(bf16[1,256,1024]{2,1,0:T(8,128)(2,1)} %param.14) | copy-start | bytes 1572868
  56.8 1.7 copy-start.1
  56.8 223.8 %all-gather.6.cloned.1.call-start = ((), (), s32[]{:S(2)}) async-start(), calls=%async_computation.4 | async-start | bytes 17825792 | tf_op jit(solution)/shard_map/all_gather | solution.py:14
  159.3 1.9 copy-start.2
  161.2 2.3 copy-start.3
  162.8 168.2 %all-gather.8.cloned.1.call-start = ((), (), s32[]{:S(2)}) async-start(), calls=%async_computation.5 | async-start | bytes 2228224 | tf_op jit(solution)/shard_map/all_gather | solution.py:141
  163.4 249.4 %reduce-scatter.5.cloned.1.call-start = ((), (), s32[]{:S(2)}) async-start(), calls=%async_computation.6 | async-start | bytes 1114112 | tf_op jit(solution)/shard_map/reduce_scatter | solution.py:144
Sparse Core Ops, SparseCore 0:
  9.1 43.8 all-gather.3
  56.9 77.4 reduce-scatter.2
  162.9 117.6 all-gather.5
  282.2 40.3 all-gather.7
  334.2 78.5 reduce-scatter.4
where the time goes:
time: 422 us; the launch traced here: 421 us
  waiting for transfers between devices  230 us (55%)
  blocking collectives  106 us (25%)
  other arithmetic  38.4 us (9%)
  local copies, waits for them, and re-layouts  19.6 us (5%)
  between operations  14 us (3%)
  matrix products  11.5 us (3%)
    reduce_scatter x1, waiting for transfers between devices, shards(): lax.psum_scatter(partial_out, 'row', scatter_dimension=1, tiled=True)  78.7 us
    reduce_scatter x1, waiting for transfers between devices, shards(): lax.psum_scatter(partial_value, 'row', scatter_dimension=1, tiled=True)  75.1 us
    all_gather x1, waiting for transfers between devices, merged(): pieces = jax.tree.map(lambda part: lax.all_gather(part, axis), value)  68.4 us
    all_gather x2, blocking collectives, merged(): pieces = jax.tree.map(lambda part: lax.all_gather(part, axis), value)  46.1 us
    psum x1, blocking collectives, shards(): squares = lax.psum(jnp.sum(features * features, axis=1), 'row')  37.7 us
    add x15, other arithmetic, pair_merge(): first[2] * first_scale[..., None] + second[2] * second_scale[..., None]  32.9 us
    all_gather x1, blocking collectives, shards(): projected_output = lax.all_gather(summed, 'row', axis=1, tiled=True)  22.6 us
    slice x3, local copies, waits for them, and re-layouts, merged(): tail = jax.tree.map(lambda part: part[1:], pieces)  14.6 us
  transfers between devices with their start and end apart: 5, of which 4 were waited for; matrix products, arithmetic and copies ran while one was open for 13% of the time, Pallas kernels for 0%

commit v1 on v0

--- a/solution.py
+++ b/solution.py
@@ -8,6 +8,7 @@
 KEY_VALUE_HEADS = 8
 HEAD_SIZE = 128
 masked_score = -1e30
+edit_the_trees = lambda vec: jnp.sum(lax.all_gather(vec, axis_name="row"), axis=0)
 
 
 def merged(value, axis, join):
@@ -48,7 +49,7 @@
     row_index = lax.axis_index("row")
     score_scale = HEAD_SIZE ** (-0.5)
     features = hidden_in.astype(jnp.float32)
-    squares = lax.psum(jnp.sum(features * features, axis=1), "row")
+    squares = edit_the_trees(jnp.sum(features * features, axis=1))
     row_scale = lax.rsqrt(squares / D + 1e-05)
     normed = (features * row_scale[:, None] * norm_gain.astype(jnp.float32)[None, :]).astype(
         jnp.bfloat16

time: 422 us -> 422 us (level)
    psum x1 -> x0, blocking collectives: 37.7 us -> none  [shards(): squares = lax.psum(jnp.sum(features * features, axis=1), 'row')]
    unnamed x0 -> x1, blocking collectives: none -> 37.7 us
  transfers between devices with their start and end apart: 5 -> 5, of which waited for: 4 -> 4; matrix products, arithmetic and copies ran while one was open for 13% -> 14% of each run, Pallas kernels for 0% -> 0%
where the time goes in v1:
time: 422 us; the launch traced here: 421 us
  waiting for transfers between devices  228 us (54%)
  blocking collectives  106 us (25%)
  other arithmetic  38.5 us (9%)
  local copies, waits for them, and re-layouts  21.2 us (5%)
  between operations  14.7 us (3%)
  matrix products  11.5 us (3%)
    reduce_scatter x1, waiting for transfers between devices, shards(): lax.psum_scatter(partial_out, 'row', scatter_dimension=1, tiled=True)  78.7 us
    reduce_scatter x1, waiting for transfers between devices, shards(): lax.psum_scatter(partial_value, 'row', scatter_dimension=1, tiled=True)  75.2 us
    all_gather x1, waiting for transfers between devices, merged(): pieces = jax.tree.map(lambda part: lax.all_gather(part, axis), value)  68.4 us
    all_gather x2, blocking collectives, merged(): pieces = jax.tree.map(lambda part: lax.all_gather(part, axis), value)  46.1 us
    unnamed x1, blocking collectives  37.7 us
    add x15, other arithmetic, pair_merge(): first[2] * first_scale[..., None] + second[2] * second_scale[..., None]  32.9 us
    all_gather x1, blocking collectives, shards(): projected_output = lax.all_gather(summed, 'row', axis=1, tiled=True)  22.6 us
    slice x3, local copies, waits for them, and re-layouts, merged(): tail = jax.tree.map(lambda part: part[1:], pieces)  14.6 us
  transfers between devices with their start and end apart: 5, of which 4 were waited for; matrix products, arithmetic and copies ran while one was open for 14% of the time, Pallas kernels for 0%

profile of v1, /device:TPU:2, one launch (start us, length us, event | category | flops | bytes accessed | tf_op | source)
XLA Modules:
  0.0 420.9 jit_solution(17388394330689839780)
XLA Ops:
  11.0 37.7 %all-reduce = f32[1024]{0:T(1024)S(1)} all-reduce(f32[1024]{0:T(1024)S(1)} %dynamic-update-slice), channel_id=2, replica_groups=mesh['row'=16,'col'=16] {'row'}, use_global_device_ids=true, to_apply=%add | all-reduce | flops 1024 | bytes 8192
  48.8 4.2 all-gather.5.cloned.1.call-done
  53.0 3.8 fusion.35
  59.3 75.2 %reduce-scatter.3.cloned.1.call-done = f32[64,384]{1,0:T(8,128)} async-done(((f32[64,6144]{1,0:T(8,128)}), f32[64,384]{1,0:T(8,128)}) %reduce-scatter.3.cloned.1.call-update) | async-done | bytes 98320 | tf_op jit(solution)/shard_map/reduce_scatter | solution.py:60
  135.4 22.6 %all_gather.36 = bf16[64,6144]{1,0:T(8,128)(2,1)S(1)} all-gather(bf16[64,384]{1,0:T(8,128)(2,1)S(1)} %convert_element_type.85), channel_id=1, replica_groups=mesh['row'=16,'col'=16] {'row'}, dimensions={1}, use_global_device_ids=true | all-gather | bytes 835584 | tf_op jit(solution)/shard_map/all_gather | solution.py:63
  165.6 24.1 %all_gather.40 = f32[16,1,32,64]{3,2,1,0:T(8,128)S(1)} all-gather(f32[1,1,32,64]{3,2,1,0:T(8,128)S(1)} %bitcast.148), channel_id=1, replica_groups=mesh['row'=16,'col'=16] {'row'}, dimensions={0}, use_global_device_ids=true | all-gather | bytes 139264 | tf_op jit(solution)/shard_map/all_gather | solution.py:15
  189.7 22.0 %all_gather.38 = f32[16,1,32,64]{3,2,1,0:T(8,128)S(1)} all-gather(f32[1,1,32,64]{3,2,1,0:T(8,128)S(1)} %bitcast.147), channel_id=1, replica_groups=mesh['row'=16,'col'=16] {'row'}, dimensions={0}, use_global_device_ids=true | all-gather | bytes 139264 | tf_op jit(solution)/shard_map/all_gather | solution.py:15
  212.3 68.4 %all-gather.7.cloned.1.call-done = f32[16,1,32,64,128]{4,3,2,1,0:T(8,128)} async-done(((f32[1,1,32,64,128]{4,3,2,1,0:T(8,128)}), f32[16,1,32,64,128]{4,3,2,1,0:T(8,128)}) %all-gather.7.cloned.1.call-update) | async-done | bytes 16777232 | tf_op jit(solution)/shard_map/all_gather | solution.py:15
  282.0 14.5 %slice.43 = f32[15,1,32,64,128]{4,3,2,1,0:T(8,128)} slice(f32[16,1,32,64,128]{4,3,2,1,0:T(8,128)} %all-gather.7.cloned.1.call-done), slice={[1:16], [0:1], [0:32], [0:64], [0:128]} | slice | bytes 31457280 | tf_op jit(solution)/shard_map/slice | solution.py:17
  296.6 34.1 %while.2 = (s32[]{:T(128)}, f32[1,32,64]{2,1,0:T(8,128)S(1)}, f32[1,32,64]{2,1,0:T(8,128)S(1)}, f32[1,32,64,128]{3,2,1,0:T(8,128)S(1)}, f32[15,1,32,64]{3,2,1,0:...) while((s32[]{:T(128)}, f32[1,32,64]{2,1,0:T(8,128)S(1)}, ...), condition=%wide.region_6.7_spmd, body=%wide.region_5.6_spmd.sunk | while | flops 800770 | bytes 3268713 | solution.py:18
  296.6 2.2 fusion.83
  298.9 2.2 fusion.83
  301.2 2.2 fusion.83
  303.5 2.2 fusion.83
  305.8 2.2 fusion.83
  308.0 2.2 fusion.83
  310.3 2.2 fusion.83
  312.6 2.2 fusion.83
  314.8 2.2 fusion.83
  317.1 2.2 fusion.83
  319.4 2.2 fusion.83
  321.7 2.2 fusion.83
  331.1 3.0 fusion.38
  334.2 78.7 %reduce-scatter.5.cloned.1.call-done = f32[64,256]{1,0:T(8,128)} async-done(((f32[64,4096]{1,0:T(8,128)}), f32[64,256]{1,0:T(8,128)}) %reduce-scatter.5.cloned.1.call-update) | async-done | bytes 65552 | tf_op jit(solution)/shard_map/reduce_scatter | solution.py:145
  (109 shorter events, 25.0 us)
Async XLA Ops:
  6.5 46.5 %all-gather.5.cloned.1.call-start = ((), (), s32[]{:S(2)}) async-start(), calls=%async_computation.2 | async-start | bytes 3342336 | tf_op jit(solution)/shard_map/all_gather | solution.py:58
  7.3 127.3 %reduce-scatter.3.cloned.1.call-start = ((), (), s32[]{:S(2)}) async-start(), calls=%async_computation.3 | async-start | bytes 1671168 | tf_op jit(solution)/shard_map/reduce_scatter | solution.py:60
  48.8 8.7 %copy-start = (bf16[1,256,1024]{2,1,0:T(8,128)(2,1)S(1)}, bf16[1,256,1024]{2,1,0:T(8,128)(2,1)}, u32[]{:S(2)}) copy-start(bf16[1,256,1024]{2,1,0:T(8,128)(2,1)} %param.14) | copy-start | bytes 1572868
  56.8 1.7 copy-start.1
  56.8 223.9 %all-gather.7.cloned.1.call-start = ((), (), s32[]{:S(2)}) async-start(), calls=%async_computation.4 | async-start | bytes 17825792 | tf_op jit(solution)/shard_map/all_gather | solution.py:15
  159.4 1.9 copy-start.2
  161.2 2.3 copy-start.3
  162.9 168.2 %all-gather.9.cloned.1.call-start = ((), (), s32[]{:S(2)}) async-start(), calls=%async_computation.5 | async-start | bytes 2228224 | tf_op jit(solution)/shard_map/all_gather | solution.py:142
  163.5 249.4 %reduce-scatter.5.cloned.1.call-start = ((), (), s32[]{:S(2)}) async-start(), calls=%async_computation.6 | async-start | bytes 1114112 | tf_op jit(solution)/shard_map/reduce_scatter | solution.py:145
Sparse Core Ops, SparseCore 0:
  9.1 43.8 all-gather.4
  56.9 77.5 reduce-scatter.2
  163.0 117.6 all-gather.6
  282.3 40.3 all-gather.8
  334.3 78.5 reduce-scatter.4
